TPU v7x, 32 devices: a whole 2x2x4 slice. The times are simulated.
32 devices in a mesh: row: 4 (over y, x), col: 8 (over z, core).
Axes of the slice: x: 2, y: 2, z: 4, core: 2. Of those that a mesh axis runs over, the one named last changes fastest.
Arguments:
- activations: bfloat16 [512, 16384], P('col', 'row'), may hold values from -6 to 6
- grad_output: bfloat16 [512, 16384], P('col', 'row'), may hold values from -6 to 6
- gate_pre: bfloat16 [512, 8192], P('row', 'col'), may hold values from -8 to 8
- up_pre: bfloat16 [512, 8192], P('row', 'col'), may hold values from -6 to 6
- w_gate: bfloat16 [16384, 8192], P('row', 'col'), may hold values from -0.046875 to 0.046875
- w_up: bfloat16 [16384, 8192], P('row', 'col'), may hold values from -0.046875 to 0.046875
- w_down: bfloat16 [8192, 16384], P('col', 'row'), may hold values from -0.0625 to 0.0625
Outputs:
- grad_input: bfloat16 [512, 16384], P('col', 'row')
- grad_gate: bfloat16 [16384, 8192], P('row', 'col')
- grad_up: bfloat16 [16384, 8192], P('row', 'col')
- grad_down: bfloat16 [8192, 16384], P('col', 'row')
All inputs are finite; a program needn't handle non-finite values.
Results may differ from a plain program's by a relative error of at most 0.005.
Values may be sent and summed in bfloat16 or wider, within the bound.
A program may use at most 128 MiB of HBM per device.

v0:
```python
import functools

import jax
import jax.numpy as jnp
from jax import lax
from jax.experimental import pallas as pl
from jax.experimental.pallas import tpu as pltpu
from jax.sharding import PartitionSpec as P

MESH = pl.DeviceIdType.MESH
CONTRACT_COLS = (((1,), (1,)), ((), ()))
CONTRACT_ROWS = (((0,), (0,)), ((), ()))
F32 = jnp.float32
BF16 = jnp.bfloat16
PIECES = 2
COLUMN_TILES = 4


def tile_of(size, want):
    tile = min(size, want)
    while size % tile:
        tile //= 2
    return tile


def exchange_kernel(
    row_size, col_size,
    act_hbm, go_hbm, gate_hbm, up_hbm, wg_hbm, wu_hbm, wd_hbm,
    gi_out, go_hbm_out, act_hbm_out, hid_hbm, ggp_hbm, gup_hbm,
    go_all, act_all, hid_all, ggp_all, gup_all,
    wd, wg, wu, gate_all, up_all, part32, part16, rs_in, gh_all, gi, pair_in, z_in, z_out,
    ld, st, go_r, go_s, pg_r, pg_s, ac_r, ac_s, pa_r, pa_s, gu_r, gu_s,
    rs_r, rs_s, ag_r, ag_s, pr_r, pr_s, z_r, z_s,
):
    R, Z = row_size, col_size // 2
    shard, width = go_hbm.shape
    rows, feats = gate_hbm.shape
    chunk = 2 * shard
    own_rows = chunk // R
    ntiles = gi.shape[0]
    wt = width // ntiles
    piece = shard // PIECES

    r = lax.axis_index("row")
    c = lax.axis_index("col")
    z, k = c // 2, c % 2
    partner = (r, c + 1 - 2 * k)
    above = (r, c + 2)
    below = (r, c - 2)
    has_up = z < Z - 1
    has_dn = z > 0

    side_len = round(R ** 0.5)
    if side_len * side_len != R:
        side_len = 1
    lines = R // side_len
    row_a, row_b = r // lines, r % lines

    def peer(d):
        return (r + d) % R

    def remote(src, dst, ssem, rsem, dev):
        return pltpu.make_async_remote_copy(
            src_ref=src, dst_ref=dst, send_sem=ssem, recv_sem=rsem, device_id=dev, device_id_type=MESH
        )

    def ds(start, size, align=None):
        return pl.ds(pl.multiple_of(start, align or size), size)

    loads = [
        pltpu.make_async_copy(go_hbm, go_all.at[c], ld.at[0]),
        pltpu.make_async_copy(gate_hbm, gate_all.at[ds(r * rows, rows), :], ld.at[1]),
        pltpu.make_async_copy(up_hbm, up_all.at[ds(r * rows, rows), :], ld.at[2]),
        pltpu.make_async_copy(wd_hbm, wd, ld.at[3]),
        pltpu.make_async_copy(act_hbm, act_all.at[c], ld.at[4]),
        pltpu.make_async_copy(wg_hbm, wg, ld.at[5]),
        pltpu.make_async_copy(wu_hbm, wu, ld.at[6]),
    ]
    for load in loads:
        load.start()

    stores = [
        pltpu.make_async_copy(src, dst, st.at[i])
        for i, (src, dst) in enumerate((
            (go_all, go_hbm_out), (hid_all, hid_hbm), (ggp_all, ggp_hbm), (gup_all, gup_hbm), (act_all, act_hbm_out)
        ))
    ]

    barrier = pltpu.get_barrier_semaphore()

    def greet(dev):
        pl.semaphore_signal(barrier, inc=1, device_id=dev, device_id_type=MESH)

    greet(partner)
    for d in range(1, R):
        greet((peer(d), c))
    pl.when(has_up)(lambda: greet(above))
    pl.when(has_dn)(lambda: greet(below))
    pl.semaphore_wait(barrier, R + jnp.where(has_up, 1, 0) + jnp.where(has_dn, 1, 0))

    def go_z(direction, j, p):
        ref = go_all.at[2 * j + k, pl.ds(p * piece, piece)]
        return remote(ref, ref, go_s.at[direction, j, p], go_r.at[j, p], (above, below)[direction])

    def go_pair(j, side):
        ref = go_all.at[2 * j + side]
        return remote(ref, ref, pg_s.at[j], pg_r.at[j], partner)

    def act_z(direction, j):
        ref = act_all.at[2 * j + k]
        return remote(ref, ref, ac_s.at[direction, j], ac_r.at[j], (above, below)[direction])

    def act_pair(j, side):
        ref = act_all.at[2 * j + side]
        return remote(ref, ref, pa_s.at[j], pa_r.at[j], partner)

    def row_all(ref, ssem, rsem, d, start, size):
        part = ref.at[ds(start, size), :]
        return remote(part, part, ssem, rsem, (peer(d), c))

    def rows_wait(ref, ssem, rsem, size):
        part = ref.at[pl.ds(0, size), :]
        return remote(part, part, ssem, rsem, (peer(1), c))

    def start_act(direction):
        act_z(direction, z).start()

    loads[0].wait()

    @pl.when(has_up)
    def _():
        for p in range(PIECES):
            go_z(0, z, p).start()

    @pl.when(has_dn)
    def _():
        for p in range(PIECES):
            go_z(1, z, p).start()

    go_pair(z, k).start()
    loads[1].wait()
    loads[2].wait()
    half = rows // 2

    def saved(ref, sems, along, owner, part, d):
        block = ref.at[ds(owner * rows + part * half, half), :]
        if along == 0:
            dev = row_a * lines + (row_b + d) % lines
        else:
            dev = (row_a + d) % side_len * lines + row_b
        return remote(block, block, sems[0], sems[1], (dev, c))

    arrays = (gate_all, up_all)
    for i, ref in enumerate(arrays):
        for d in range(1, lines):
            saved(ref, (gu_s.at[i, 0], gu_r.at[i, 0]), 0, r, 0, d).start()
        for d in range(1, side_len):
            saved(ref, (gu_s.at[i, 1], gu_r.at[i, 1]), 1, r, 1, d).start()
    for i, ref in enumerate(arrays):
        for d in range(1, side_len):
            saved(ref, (gu_s.at[i, 2], gu_r.at[i, 2]), 1, r, 0, d).start()
        for d in range(1, lines):
            saved(ref, (gu_s.at[i, 3], gu_r.at[i, 3]), 0, r, 1, d).start()

    def saved_wait(i, stage, count):
        part = arrays[i].at[pl.ds(0, count * half), :]
        return remote(part, part, gu_s.at[i, stage], gu_r.at[i, stage], partner)

    def forward_saved():
        for i, ref in enumerate(arrays):
            if lines > 1:
                saved_wait(i, 0, lines - 1).wait_recv()
            for e in range(1, lines):
                owner = row_a * lines + (row_b + e) % lines
                for d in range(1, side_len):
                    saved(ref, (gu_s.at[i, 4], gu_r.at[i, 4]), 1, owner, 0, d).start()
            if side_len > 1:
                saved_wait(i, 1, side_len - 1).wait_recv()
            for e in range(1, side_len):
                owner = (row_a + e) % side_len * lines + row_b
                for d in range(1, lines):
                    saved(ref, (gu_s.at[i, 5], gu_r.at[i, 5]), 0, owner, 1, d).start()

    counts = (
        lines - 1, side_len - 1, side_len - 1, lines - 1,
        (lines - 1) * (side_len - 1), (lines - 1) * (side_len - 1),
    )
    loads[4].wait()
    act_pair(z, k).start()
    pl.when(has_up & (z == 0))(lambda: start_act(0))
    pl.when(has_dn & (z == Z - 1))(lambda: start_act(1))

    def forward(s):
        for p in range(PIECES):
            @pl.when(z - s >= 0)
            def _():
                j = z - s
                go_z(0, j, p).wait_recv()
                pl.when(has_up)(lambda: go_z(0, j, p).start())
                if p == PIECES - 1:
                    go_pair(j, k).start()
                    pl.when(has_up & (s == z))(lambda: start_act(0))

            @pl.when(z + s < Z)
            def _():
                j = z + s
                go_z(1, j, p).wait_recv()
                pl.when(has_dn)(lambda: go_z(1, j, p).start())
                if p == PIECES - 1:
                    go_pair(j, k).start()
                    pl.when(has_dn & (s == Z - 1 - z))(lambda: start_act(1))

    def act_forward(s):
        @pl.when(z - s >= 0)
        def _():
            j = z - s
            act_z(0, j).wait_recv()
            pl.when(has_up)(lambda: act_z(0, j).start())
            act_pair(j, k).start()

        @pl.when(z + s < Z)
        def _():
            j = z + s
            act_z(1, j).wait_recv()
            pl.when(has_dn)(lambda: act_z(1, j).start())
            act_pair(j, k).start()

    ftile = tile_of(feats, 256)

    def partial_hidden(j):
        go_pair(j, 1 - k).wait_recv()
        lhs = go_all[pl.ds(2 * j, 2)].reshape(chunk, width)

        @pl.loop(0, feats // ftile)
        def _(f):
            cols = ds(f * ftile, ftile)
            res = lax.dot_general(lhs, wd[cols, :], CONTRACT_COLS, preferred_element_type=F32)
            part32[ds(j * chunk, chunk), cols] = res
            part16[ds(j * chunk, chunk), cols] = res.astype(BF16)

        for d in range(1, R):
            src = part16.at[ds(j * chunk + peer(d) * own_rows, own_rows), :]
            dst = rs_in.at[ds((j * (R - 1) + d - 1) * own_rows, own_rows), :]
            remote(src, dst, rs_s.at[j], rs_r.at[j], (peer(d), c)).start()

    def finish_sum(j):
        rows_wait(rs_in, rs_s.at[j], rs_r.at[j], (R - 1) * own_rows).wait_recv()
        mine = ds(j * chunk + r * own_rows, own_rows)
        total = part32[mine, :]
        for d in range(1, R):
            total = total + rs_in[ds((j * (R - 1) + d - 1) * own_rows, own_rows), :].astype(F32)
        gh_all[mine, :] = total.astype(BF16)
        for d in range(1, R):
            row_all(gh_all, ag_s.at[j], ag_r.at[j], d, j * chunk + r * own_rows, own_rows).start()

    eblock = 16

    def finish_gather(j):
        rows_wait(gh_all, ag_s.at[j], ag_r.at[j], (R - 1) * own_rows).wait_recv()

        @pl.loop(0, chunk // eblock)
        def _(b):
            at = pl.ds(pl.multiple_of(j * chunk + b * eblock, eblock), eblock)
            gate = gate_all[at, :].astype(F32)
            up = up_all[at, :].astype(F32)
            grad = gh_all[at, :].astype(F32)
            sigma = 1.0 / (1.0 + jnp.exp(-gate))
            hid_all[at, :] = (gate * sigma * up).astype(BF16)
            ggp_all[at, :] = (grad * up * sigma * (1.0 + gate * (1.0 - sigma))).astype(BF16)
            gup_all[at, :] = (grad * gate * sigma).astype(BF16)

    def gathered_saved():
        for i in range(2):
            for stage in range(2, 6):
                if counts[stage]:
                    saved_wait(i, stage, counts[stage]).wait_recv()

    def at_distance(s, step):
        pl.when(z - s >= 0)(lambda: step(z - s))
        if s > 0:
            pl.when(z + s < Z)(lambda: step(z + s))

    for s in range(Z):
        if s > 0:
            forward(s)
        if s == 1:
            forward_saved()
        if s == 0:
            loads[3].wait()
        at_distance(s, partial_hidden)
        if s == Z - 1:
            act_forward(1)
        if s >= 1:
            at_distance(s - 1, finish_sum)
        if s == 2:
            gathered_saved()
        if s >= 2:
            at_distance(s - 2, finish_gather)
    if Z == 1:
        forward_saved()
    if Z <= 2:
        gathered_saved()
    at_distance(Z - 1, finish_sum)
    stores[0].start()
    if Z > 1:
        at_distance(Z - 2, finish_gather)
    at_distance(Z - 1, finish_gather)
    for store in stores[1:4]:
        store.start()

    loads[5].wait()
    loads[6].wait()
    gtile = tile_of(wt, 256)

    def input_tile(n):
        @pl.loop(0, wt // gtile)
        def _(t):
            at = ds(n * wt + t * gtile, gtile)
            res = lax.dot_general(ggp_all[...], wg[at, :], CONTRACT_COLS, preferred_element_type=F32)
            res = res + lax.dot_general(gup_all[...], wu[at, :], CONTRACT_COLS, preferred_element_type=F32)
            for j in range(Z):
                for side in range(2):
                    low_row = (2 * j + side) * shard
                    gi[n, side, j, :, ds(t * gtile, gtile)] = res[low_row : low_row + shard]

        pair_sum(n).start()

    def pair_sum(n):
        return remote(gi.at[n, 1 - k], pair_in.at[n], pr_s.at[n], pr_r.at[n], partner)

    def z_copy(n, j, slot, dev):
        return remote(z_out.at[n, j], z_in.at[n, slot], z_s.at[n, j], z_r.at[n, slot], dev)

    def pass_on(n, j, has_more, slot, dev):
        total = gi[n, k, j] + pair_in[n, j]

        @pl.when(has_more)
        def _():
            z_copy(n, j, j, dev).wait_recv()
            z_out[n, j] = (total + z_in[n, j].astype(F32)).astype(BF16)

        @pl.when(jnp.logical_not(has_more))
        def _():
            z_out[n, j] = total.astype(BF16)

        z_copy(n, j, slot, dev).start()

    lower = 2 * z < Z

    def serve_up(n, side):
        for j in range(Z - 1, 0, -1):
            pl.when((z < j) & (lower == side))(functools.partial(pass_on, n, j, has_dn, j, above))

    def serve(n):
        pair_sum(n).wait_recv()
        serve_up(n, True)
        for j in range(Z - 1):
            slot = jnp.where(z - 1 == j, Z, j)
            pl.when(z > j)(functools.partial(pass_on, n, j, has_up, slot, below))
        serve_up(n, False)

    def finish(n):
        total = gi[n, k, z] + pair_in[n, z]
        cols = pl.ds(n * wt, wt)
        gi[n, k, z] = total

        @pl.when(has_dn)
        def _():
            z_copy(n, z, z, below).wait_recv()
            gi[n, k, z] += z_in[n, z].astype(F32)

        @pl.when(has_up)
        def _():
            z_copy(n, z, Z, above).wait_recv()
            gi[n, k, z] += z_in[n, Z].astype(F32)

        gi_out[:, cols] = gi[n, k, z].astype(BF16)

    for n in range(ntiles):
        input_tile(n)
        if n >= 1:
            serve(n - 1)
        if n + 2 < Z and n >= 0:
            act_forward(n + 2)
    serve(ntiles - 1)
    for s in range(ntiles + 2, Z):
        act_forward(s)
    for n in range(ntiles):
        finish(n)

    for j in range(Z):
        act_pair(j, 1 - k).wait_recv()
    stores[4].start()
    for store in stores:
        store.wait()
    for j in range(Z):
        go_pair(j, k).wait_send()
        act_pair(j, k).wait_send()
        rows_wait(part16, rs_s.at[j], rs_r.at[j], (R - 1) * own_rows).wait_send()
        rows_wait(gh_all, ag_s.at[j], ag_r.at[j], (R - 1) * own_rows).wait_send()

        @pl.when((z >= j) & has_up)
        def _():
            for p in range(PIECES):
                go_z(0, j, p).wait_send()
            act_z(0, j).wait_send()

        @pl.when((z <= j) & has_dn)
        def _():
            for p in range(PIECES):
                go_z(1, j, p).wait_send()
            act_z(1, j).wait_send()

        @pl.when(z != j)
        def _():
            for n in range(ntiles):
                z_copy(n, j, j, partner).wait_send()

    for i in range(2):
        for stage in range(6):
            if counts[stage]:
                saved_wait(i, stage, counts[stage]).wait_send()
    for n in range(ntiles):
        pair_sum(n).wait_send()


def exchange(row_size, col_size, act, go, gate, up, wg, wu, wd):
    R, Z = row_size, col_size // 2
    shard, width = go.shape
    rows, feats = gate.shape
    tokens = shard * col_size
    own_rows = 2 * shard // R
    nt = COLUMN_TILES
    wt = width // nt
    hbm = pl.BlockSpec(memory_space=pltpu.HBM)
    vmem = pl.BlockSpec(memory_space=pltpu.VMEM)
    dma = pltpu.SemaphoreType.DMA
    sds = jax.ShapeDtypeStruct
    return pl.pallas_call(
        functools.partial(exchange_kernel, row_size, col_size),
        out_shape=[
            sds((shard, width), BF16),
            sds((col_size, shard, width), BF16),
            sds((col_size, shard, width), BF16),
            sds((tokens, feats), BF16),
            sds((tokens, feats), BF16),
            sds((tokens, feats), BF16),
        ],
        in_specs=[hbm] * 7,
        out_specs=[vmem] + [hbm] * 5,
        scratch_shapes=[
            pltpu.VMEM((col_size, shard, width), BF16),
            pltpu.VMEM((col_size, shard, width), BF16),
            pltpu.VMEM((tokens, feats), BF16),
            pltpu.VMEM((tokens, feats), BF16),
            pltpu.VMEM((tokens, feats), BF16),
            pltpu.VMEM(wd.shape, BF16),
            pltpu.VMEM(wg.shape, BF16),
            pltpu.VMEM(wu.shape, BF16),
            pltpu.VMEM((tokens, feats), BF16),
            pltpu.VMEM((tokens, feats), BF16),
            pltpu.VMEM((tokens, feats), F32),
            pltpu.VMEM((tokens, feats), BF16),
            pltpu.VMEM((Z * (R - 1) * own_rows, feats), BF16),
            pltpu.VMEM((tokens, feats), BF16),
            pltpu.VMEM((nt, 2, Z, shard, wt), F32),
            pltpu.VMEM((nt, Z, shard, wt), F32),
            pltpu.VMEM((nt, Z + 1, shard, wt), BF16),
            pltpu.VMEM((nt, Z, shard, wt), BF16),
            dma((7,)), dma((5,)),
            dma((Z, PIECES)), dma((2, Z, PIECES)), dma((Z,)), dma((Z,)),
            dma((Z,)), dma((2, Z)), dma((Z,)), dma((Z,)),
            dma((2, 6)), dma((2, 6)),
            dma((Z,)), dma((Z,)), dma((Z,)), dma((Z,)),
            dma((nt,)), dma((nt,)), dma((nt, Z + 1)), dma((nt, Z)),
        ],
        compiler_params=pltpu.CompilerParams(
            collective_id=0, has_side_effects=True, vmem_limit_bytes=67043328
        ),
        name="exchange",
    )(act, go, gate, up, wg, wu, wd)


def grads_kernel(tiles, lhs1, rhs1, lhs2, lhs3, rhs2, out1, out2, out3):
    i = pl.program_id(0)
    tokens = lhs1.shape[0]

    def product(lhs, rhs):
        return lax.dot_general(lhs, rhs, CONTRACT_ROWS, preferred_element_type=F32).astype(BF16)

    out1[...] = product(lhs1[...], rhs1[...].reshape(tokens, rhs1.shape[2]))
    rhs = rhs2[...].reshape(tokens, rhs2.shape[2])
    out2[...] = product(rhs, lhs2[...])
    out3[...] = product(rhs, lhs3[...])


def weight_grads(hid, go, act, ggp, gup):
    tokens, feats = hid.shape
    cols, shard, width = go.shape
    steps = min(8, feats // 128, width // 128)
    ft, wt = feats // steps, width // steps
    sds = jax.ShapeDtypeStruct
    vmem = pl.BlockSpec(memory_space=pltpu.VMEM)
    return pl.pallas_call(
        functools.partial(grads_kernel, steps),
        grid=(steps,),
        out_shape=[sds((feats, width), BF16), sds((width, feats), BF16), sds((width, feats), BF16)],
        in_specs=[
            pl.BlockSpec((tokens, ft), lambda i: (0, i)),
            pl.BlockSpec((cols, shard, width), lambda i: (0, 0, 0)),
            pl.BlockSpec((tokens, feats), lambda i: (0, 0)),
            pl.BlockSpec((tokens, feats), lambda i: (0, 0)),
            pl.BlockSpec((cols, shard, wt), lambda i: (0, 0, i)),
        ],
        out_specs=[
            pl.BlockSpec((ft, width), lambda i: (i, 0)),
            pl.BlockSpec((wt, feats), lambda i: (i, 0)),
            pl.BlockSpec((wt, feats), lambda i: (i, 0)),
        ],
        name="weight_grads",
    )(hid, go, ggp, gup, act)


def local(row_size, col_size, activations, grad_output, gate_pre, up_pre, w_gate, w_up, w_down):
    grad_input, go_all, act_all, hid, ggp, gup = exchange(
        row_size, col_size, activations, grad_output, gate_pre, up_pre, w_gate, w_up, w_down
    )
    grad_down, grad_gate, grad_up = weight_grads(hid, go_all, act_all, ggp, gup)
    return grad_input, grad_gate, grad_up, grad_down


def solution(mesh):
    in_specs = (
        P("col", "row"), P("col", "row"), P("row", "col"), P("row", "col"),
        P("row", "col"), P("row", "col"), P("col", "row"),
    )
    out_specs = (P("col", "row"), P("row", "col"), P("row", "col"), P("col", "row"))
    body = functools.partial(local, mesh.shape["row"], mesh.shape["col"])
    return jax.shard_map(body, mesh=mesh, in_specs=in_specs, out_specs=out_specs, check_vma=False)
```

profile of v0, /device:TPU:0, one launch (start us, length us, event | category | flops | bytes accessed | tf_op | source)
XLA Modules:
  0.0 132.5 jit_solution(11436107664007790551)
XLA Ops:
  0.6 112.0 %exchange.1 = (bf16[64,4096]{1,0:T(8,128)(2,1)}, bf16[8,64,4096]{2,1,0:T(8,128)(2,1)}, bf16[8,64,4096]{2,1,0:T(8,128)(2,1)}, bf16[512,1024]{1,0:T(8,128)(2,1)}, ...) custom-call(bf16[64,4096]{1,0:T(8,128)(2,1)} %act_hbm.1, bf16[64,4096]{1,0:T(8,128)(2,1)} %go_hbm.1, ...), custom_call_target="tpu_custom_call" | custom-call | tf_op jit(solution)/shard_map/exchange/pallas_call | solution.py:439
  112.7 0.0 copy-start
  112.7 19.0 %weight_grads.1 = (bf16[1024,4096]{1,0:T(8,128)(2,1)}, bf16[4096,1024]{1,0:T(8,128)(2,1)}, bf16[4096,1024]{1,0:T(8,128)(2,1)}) custom-call(bf16[512,1024]{1,0:T(8,128)(2,1)} %get-tuple-element.14.lhs1, bf16[8,64,4096]{2,1,0:T(8,128)(2,1)} %get-tuple-element.15.rhs1, bf16[512,1024]{1,0:T(8,128)(2,1)} %get-tuple-element.16.lhs2, ...), custom_call_target="tpu_custom_call" | custom-call | tf_op jit(solution)/shard_map/weight_grads/pallas_call | solution.py:504
  131.7 0.0 copy-done
  131.7 0.8 copy.12
Async XLA Ops:
  112.7 19.0 %copy-start = (bf16[64,4096]{1,0:T(8,128)(2,1)S(1)}, bf16[64,4096]{1,0:T(8,128)(2,1)}, u32[]{:S(2)}) copy-start(bf16[64,4096]{1,0:T(8,128)(2,1)} %get-tuple-element.26) | copy-start | bytes 1572868
where the time goes:
time: 133 us; the launch traced here: 132 us
  Pallas kernels  131 us (98%)
    pallas_call x1, Pallas kernels, exchange(): pl.pallas_call(functools.partial(exchange_kernel, row_size, col_size), ou...  112 us
    pallas_call x1, Pallas kernels, weight_grads(): pl.pallas_call(functools.partial(grads_kernel, steps), grid=(steps,), out...  19 us

commit v1 on v0

--- a/solution.py
+++ b/solution.py
@@ -26,10 +26,10 @@
 def exchange_kernel(
     row_size, col_size,
     act_hbm, go_hbm, gate_hbm, up_hbm, wg_hbm, wu_hbm, wd_hbm,
-    gi_out, go_hbm_out, act_hbm_out, hid_hbm, ggp_hbm, gup_hbm,
-    go_all, act_all, hid_all, ggp_all, gup_all,
-    wd, wg, wu, gate_all, up_all, part32, part16, rs_in, gh_all, gi, pair_in, z_in, z_out,
-    ld, st, go_r, go_s, pg_r, pg_s, ac_r, ac_s, pa_r, pa_s, gu_r, gu_s,
+    gi_out, wd, wg, act_all, gup_all,
+    go_all, hid_all, ggp_all,
+    wu, gate_all, up_all, part32, own32, part16, rs_in, gh_all, gi, pair_in, z_in, z_out,
+    ld, go_r, go_s, pg_r, pg_s, ac_r, ac_s, pa_r, pa_s, gu_r, gu_s,
     rs_r, rs_s, ag_r, ag_s, pr_r, pr_s, z_r, z_s,
 ):
     R, Z = row_size, col_size // 2
@@ -37,6 +37,7 @@
     rows, feats = gate_hbm.shape
     chunk = 2 * shard
     own_rows = chunk // R
+    tokens = chunk * Z
     ntiles = gi.shape[0]
     wt = width // ntiles
     piece = shard // PIECES
@@ -78,13 +79,6 @@
     ]
     for load in loads:
         load.start()
-
-    stores = [
-        pltpu.make_async_copy(src, dst, st.at[i])
-        for i, (src, dst) in enumerate((
-            (go_all, go_hbm_out), (hid_all, hid_hbm), (ggp_all, ggp_hbm), (gup_all, gup_hbm), (act_all, act_hbm_out)
-        ))
-    ]
 
     barrier = pltpu.get_barrier_semaphore()
 
@@ -210,20 +204,29 @@
                     go_pair(j, k).start()
                     pl.when(has_dn & (s == Z - 1 - z))(lambda: start_act(1))
 
-    def act_forward(s):
-        @pl.when(z - s >= 0)
-        def _():
-            j = z - s
-            act_z(0, j).wait_recv()
-            pl.when(has_up)(lambda: act_z(0, j).start())
-            act_pair(j, k).start()
-
-        @pl.when(z + s < Z)
-        def _():
-            j = z + s
-            act_z(1, j).wait_recv()
-            pl.when(has_dn)(lambda: act_z(1, j).start())
-            act_pair(j, k).start()
+    def act_from(direction, j, relay):
+        act_z(direction, j).wait_recv()
+        if relay:
+            act_z(direction, j).start()
+        act_pair(j, k).start()
+
+    to_edge = jnp.minimum(z, Z - 1 - z)
+    lower = 2 * z < Z
+    edge = to_edge == 0
+
+    def act_relay(t):
+        near = t - to_edge
+        far = t - (Z - 1 - to_edge)
+        near_ok = (near >= 1) & (near <= to_edge)
+        far_ok = (far >= 1) & (far <= Z - 1 - to_edge) & jnp.logical_not(edge)
+        pl.when(near_ok & lower)(lambda: act_from(0, z - near, True))
+        pl.when(near_ok & jnp.logical_not(lower))(lambda: act_from(1, z + near, True))
+        pl.when(far_ok & lower)(lambda: act_from(1, z + far, True))
+        pl.when(far_ok & jnp.logical_not(lower))(lambda: act_from(0, z - far, True))
+
+    def act_end(s):
+        pl.when(edge & (z - s >= 0))(lambda: act_from(0, z - s, False))
+        pl.when(edge & (z + s < Z))(lambda: act_from(1, z + s, False))
 
     ftile = tile_of(feats, 256)
 
@@ -235,9 +238,10 @@
         def _(f):
             cols = ds(f * ftile, ftile)
             res = lax.dot_general(lhs, wd[cols, :], CONTRACT_COLS, preferred_element_type=F32)
-            part32[ds(j * chunk, chunk), cols] = res
+            part32[:, cols] = res
             part16[ds(j * chunk, chunk), cols] = res.astype(BF16)
 
+        own32[ds(j * own_rows, own_rows), :] = part32[ds(r * own_rows, own_rows), :]
         for d in range(1, R):
             src = part16.at[ds(j * chunk + peer(d) * own_rows, own_rows), :]
             dst = rs_in.at[ds((j * (R - 1) + d - 1) * own_rows, own_rows), :]
@@ -246,7 +250,7 @@
     def finish_sum(j):
         rows_wait(rs_in, rs_s.at[j], rs_r.at[j], (R - 1) * own_rows).wait_recv()
         mine = ds(j * chunk + r * own_rows, own_rows)
-        total = part32[mine, :]
+        total = own32[ds(j * own_rows, own_rows), :]
         for d in range(1, R):
             total = total + rs_in[ds((j * (R - 1) + d - 1) * own_rows, own_rows), :].astype(F32)
         gh_all[mine, :] = total.astype(BF16)
@@ -283,81 +287,103 @@
     for s in range(Z):
         if s > 0:
             forward(s)
-        if s == 1:
-            forward_saved()
         if s == 0:
             loads[3].wait()
         at_distance(s, partial_hidden)
-        if s == Z - 1:
-            act_forward(1)
-        if s >= 1:
-            at_distance(s - 1, finish_sum)
+        if s == 1:
+            forward_saved()
+        if s >= 2:
+            act_relay(s)
+        if s > 0:
+            pl.when(jnp.logical_not(edge))(lambda: at_distance(s - 1, finish_sum))
         if s == 2:
             gathered_saved()
-        if s >= 2:
-            at_distance(s - 2, finish_gather)
-    if Z == 1:
-        forward_saved()
-    if Z <= 2:
+            at_distance(0, finish_gather)
+            pl.when(edge)(lambda: at_distance(1, finish_gather))
+        if s > 2:
+            pl.when(jnp.logical_not(edge))(lambda: at_distance(s - 2, finish_gather))
+            pl.when(edge)(lambda: at_distance(s - 1, finish_gather))
+        if s < Z - 1:
+            pl.when(edge)(lambda: at_distance(s, finish_sum))
+    if Z == 2:
         gathered_saved()
-    at_distance(Z - 1, finish_sum)
-    stores[0].start()
-    if Z > 1:
-        at_distance(Z - 2, finish_gather)
-    at_distance(Z - 1, finish_gather)
-    for store in stores[1:4]:
-        store.start()
+        at_distance(0, finish_gather)
+    if Z > 2:
+        pl.when(jnp.logical_not(edge))(lambda: at_distance(Z - 2, finish_gather))
 
     loads[5].wait()
     loads[6].wait()
     gtile = tile_of(wt, 256)
 
-    def input_tile(n):
+    first = jnp.where(lower, 0, 1)
+    last = jnp.where(lower, Z - 1, 0)
+
+    def input_tile(n, start, count):
+        rows_at = ds(start * chunk, count * chunk, chunk)
+
         @pl.loop(0, wt // gtile)
         def _(t):
             at = ds(n * wt + t * gtile, gtile)
-            res = lax.dot_general(ggp_all[...], wg[at, :], CONTRACT_COLS, preferred_element_type=F32)
-            res = res + lax.dot_general(gup_all[...], wu[at, :], CONTRACT_COLS, preferred_element_type=F32)
-            for j in range(Z):
+            res = lax.dot_general(ggp_all[rows_at, :], wg[at, :], CONTRACT_COLS, preferred_element_type=F32)
+            res = res + lax.dot_general(gup_all[rows_at, :], wu[at, :], CONTRACT_COLS, preferred_element_type=F32)
+            for j in range(count):
                 for side in range(2):
                     low_row = (2 * j + side) * shard
-                    gi[n, side, j, :, ds(t * gtile, gtile)] = res[low_row : low_row + shard]
-
-        pair_sum(n).start()
-
-    def pair_sum(n):
-        return remote(gi.at[n, 1 - k], pair_in.at[n], pr_s.at[n], pr_r.at[n], partner)
+                    gi[n, side, start + j, :, ds(t * gtile, gtile)] = res[low_row : low_row + shard]
+
+    def pair_sum(n, late):
+        at = pl.ds(last, 1) if late else pl.ds(first, Z - 1)
+        return remote(gi.at[n, 1 - k, at], pair_in.at[n, at], pr_s.at[late, n], pr_r.at[late, n], partner)
+
+    def early(n):
+        input_tile(n, first, Z - 1)
+        pair_sum(n, 0).start()
+
+    def late(n):
+        input_tile(n, last, 1)
+        pair_sum(n, 1).start()
 
     def z_copy(n, j, slot, dev):
         return remote(z_out.at[n, j], z_in.at[n, slot], z_s.at[n, j], z_r.at[n, slot], dev)
 
-    def pass_on(n, j, has_more, slot, dev):
+    def pass_on(n, j, fed, slot, dev):
         total = gi[n, k, j] + pair_in[n, j]
-
-        @pl.when(has_more)
-        def _():
+        if fed:
             z_copy(n, j, j, dev).wait_recv()
-            z_out[n, j] = (total + z_in[n, j].astype(F32)).astype(BF16)
-
-        @pl.when(jnp.logical_not(has_more))
-        def _():
-            z_out[n, j] = total.astype(BF16)
-
+            total = total + z_in[n, j].astype(F32)
+        z_out[n, j] = total.astype(BF16)
         z_copy(n, j, slot, dev).start()
 
-    lower = 2 * z < Z
-
-    def serve_up(n, side):
-        for j in range(Z - 1, 0, -1):
-            pl.when((z < j) & (lower == side))(functools.partial(pass_on, n, j, has_dn, j, above))
-
-    def serve(n):
-        pair_sum(n).wait_recv()
-        serve_up(n, True)
-        for j in range(Z - 1):
-            slot = jnp.where(z - 1 == j, Z, j)
-            pl.when(z > j)(functools.partial(pass_on, n, j, has_up, slot, below))
-        serve_up(n, False)
+    def move_up(n, j, fed):
+        pass_on(n, j, fed, j, above)
+
+    def move_down(n, j, fed):
+        pass_on(n, j, fed, jnp.where(z - 1 == j, Z, j), below)
+
+    def edge_serve(n, is_late):
+        pair_sum(n, is_late).wait_recv()
+        for j in [Z - 1] if is_late else range(Z - 2, 0, -1):
+            pl.when(lower)(functools.partial(move_up, n, j, False))
+        for j in [0] if is_late else range(1, Z - 1):
+            pl.when(jnp.logical_not(lower))(functools.partial(move_down, n, j, False))
+
+    def mid_early(n):
+        pair_sum(n, 0).wait_recv()
+
+        def ups(side):
+            for j in range(Z - 2, 1, -1):
+                pl.when((z < j) & (lower == side))(functools.partial(move_up, n, j, True))
+
+        ups(True)
+        for j in range(1, Z - 2):
+            pl.when(z > j)(functools.partial(move_down, n, j, True))
+        ups(False)
+
+    def mid_late(n, near):
+        if near:
+            pair_sum(n, 1).wait_recv()
+        pl.when(lower == near)(functools.partial(move_up, n, Z - 1, True))
+        pl.when(lower != near)(functools.partial(move_down, n, 0, True))
 
     def finish(n):
         total = gi[n, k, z] + pair_in[n, z]
@@ -376,23 +402,91 @@
 
         gi_out[:, cols] = gi[n, k, z].astype(BF16)
 
-    for n in range(ntiles):
-        input_tile(n)
-        if n >= 1:
-            serve(n - 1)
-        if n + 2 < Z and n >= 0:
-            act_forward(n + 2)
-    serve(ntiles - 1)
-    for s in range(ntiles + 2, Z):
-        act_forward(s)
+    blocks = 4
+    fb = feats // blocks
+    wb = width // blocks
+    nb = tile_of(width, 1024)
+
+    def down_block(i):
+        rows_at = pl.ds(i * fb, fb)
+
+        @pl.loop(0, width // nb)
+        def _(t):
+            cols = ds(t * nb, nb)
+            rhs = go_all[:, :, cols].reshape(tokens, nb)
+            wd[rows_at, cols] = lax.dot_general(
+                hid_all[:, rows_at], rhs, CONTRACT_ROWS, preferred_element_type=F32
+            ).astype(BF16)
+
+    def gate_block(i):
+        gb = tile_of(wb, 256)
+
+        @pl.loop(0, wb // gb)
+        def _(t):
+            cols = ds(i * wb + t * gb, gb)
+            lhs = act_all[:, :, cols].reshape(tokens, gb)
+            wg[cols, :] = lax.dot_general(
+                lhs, ggp_all[...], CONTRACT_ROWS, preferred_element_type=F32
+            ).astype(BF16)
+
+    early(0)
+
+    @pl.when(edge)
+    def _():
+        edge_serve(0, 0)
+        at_distance(Z - 1, finish_sum)
+        early(1)
+        at_distance(Z - 1, finish_gather)
+        late(0)
+        for n in range(1, ntiles):
+            edge_serve(n, 0)
+            edge_serve(n - 1, 1)
+            if n + 1 < ntiles:
+                early(n + 1)
+            late(n)
+        edge_serve(ntiles - 1, 1)
+
+    @pl.when(jnp.logical_not(edge))
+    def _():
+        at_distance(Z - 1, finish_sum)
+        mid_early(0)
+        act_relay(Z)
+        early(1)
+        at_distance(Z - 1, finish_gather)
+        late(0)
+        for n in range(1, ntiles):
+            if n + 1 < ntiles:
+                early(n + 1)
+            mid_early(n)
+            late(n)
+            down_block(n - 1)
+            mid_late(n - 1, True)
+            if n > 1:
+                mid_late(n - 2, False)
+            act_relay(Z + n)
+        for n in (ntiles - 1, ntiles):
+            if n < ntiles:
+                down_block(n)
+                mid_late(n, True)
+            mid_late(n - 1, False)
+        for t in range(Z + ntiles, 2 * Z - 2):
+            act_relay(t)
+
+    for s in range(1, Z):
+        act_end(s)
+    for j in range(Z):
+        act_pair(j, 1 - k).wait_recv()
+
+    @pl.when(edge)
+    def _():
+        for i in range(blocks):
+            down_block(i)
+
     for n in range(ntiles):
         finish(n)
-
-    for j in range(Z):
-        act_pair(j, 1 - k).wait_recv()
-    stores[4].start()
-    for store in stores:
-        store.wait()
+        for i in range(n * blocks // ntiles, (n + 1) * blocks // ntiles):
+            gate_block(i)
+
     for j in range(Z):
         go_pair(j, k).wait_send()
         act_pair(j, k).wait_send()
@@ -421,7 +515,8 @@
             if counts[stage]:
                 saved_wait(i, stage, counts[stage]).wait_send()
     for n in range(ntiles):
-        pair_sum(n).wait_send()
+        pair_sum(n, 0).wait_send()
+        pair_sum(n, 1).wait_send()
 
 
 def exchange(row_size, col_size, act, go, gate, up, wg, wu, wd):
@@ -440,26 +535,22 @@
         functools.partial(exchange_kernel, row_size, col_size),
         out_shape=[
             sds((shard, width), BF16),
-            sds((col_size, shard, width), BF16),
-            sds((col_size, shard, width), BF16),
-            sds((tokens, feats), BF16),
-            sds((tokens, feats), BF16),
-            sds((tokens, feats), BF16),
+            pltpu.VMEM(wd.shape, BF16),
+            pltpu.VMEM(wg.shape, BF16),
+            pltpu.VMEM((col_size, shard, width), BF16),
+            pltpu.VMEM((tokens, feats), BF16),
         ],
         in_specs=[hbm] * 7,
-        out_specs=[vmem] + [hbm] * 5,
+        out_specs=[vmem] * 5,
         scratch_shapes=[
-            pltpu.VMEM((col_size, shard, width), BF16),
             pltpu.VMEM((col_size, shard, width), BF16),
             pltpu.VMEM((tokens, feats), BF16),
             pltpu.VMEM((tokens, feats), BF16),
-            pltpu.VMEM((tokens, feats), BF16),
-            pltpu.VMEM(wd.shape, BF16),
-            pltpu.VMEM(wg.shape, BF16),
             pltpu.VMEM(wu.shape, BF16),
             pltpu.VMEM((tokens, feats), BF16),
             pltpu.VMEM((tokens, feats), BF16),
-            pltpu.VMEM((tokens, feats), F32),
+            pltpu.VMEM((2 * shard, feats), F32),
+            pltpu.VMEM((Z * own_rows, feats), F32),
             pltpu.VMEM((tokens, feats), BF16),
             pltpu.VMEM((Z * (R - 1) * own_rows, feats), BF16),
             pltpu.VMEM((tokens, feats), BF16),
@@ -467,65 +558,73 @@
             pltpu.VMEM((nt, Z, shard, wt), F32),
             pltpu.VMEM((nt, Z + 1, shard, wt), BF16),
             pltpu.VMEM((nt, Z, shard, wt), BF16),
-            dma((7,)), dma((5,)),
+            dma((7,)),
             dma((Z, PIECES)), dma((2, Z, PIECES)), dma((Z,)), dma((Z,)),
             dma((Z,)), dma((2, Z)), dma((Z,)), dma((Z,)),
             dma((2, 6)), dma((2, 6)),
             dma((Z,)), dma((Z,)), dma((Z,)), dma((Z,)),
-            dma((nt,)), dma((nt,)), dma((nt, Z + 1)), dma((nt, Z)),
+            dma((2, nt)), dma((2, nt)), dma((nt, Z + 1)), dma((nt, Z)),
         ],
         compiler_params=pltpu.CompilerParams(
-            collective_id=0, has_side_effects=True, vmem_limit_bytes=67043328
+            collective_id=0, has_side_effects=True, vmem_limit_bytes=39 << 20
         ),
         name="exchange",
-    )(act, go, gate, up, wg, wu, wd)
-
-
-def grads_kernel(tiles, lhs1, rhs1, lhs2, lhs3, rhs2, out1, out2, out3):
+    )(*(pltpu.with_memory_space_constraint(x, pltpu.HBM) for x in (act, go, gate, up, wg, wu, wd)))
+
+
+def last_kernel(steps, lhs, rhs, down, gate, out, down_out, gate_out, sems):
     i = pl.program_id(0)
-    tokens = lhs1.shape[0]
-
-    def product(lhs, rhs):
-        return lax.dot_general(lhs, rhs, CONTRACT_ROWS, preferred_element_type=F32).astype(BF16)
-
-    out1[...] = product(lhs1[...], rhs1[...].reshape(tokens, rhs1.shape[2]))
-    rhs = rhs2[...].reshape(tokens, rhs2.shape[2])
-    out2[...] = product(rhs, lhs2[...])
-    out3[...] = product(rhs, lhs3[...])
-
-
-def weight_grads(hid, go, act, ggp, gup):
-    tokens, feats = hid.shape
-    cols, shard, width = go.shape
-    steps = min(8, feats // 128, width // 128)
-    ft, wt = feats // steps, width // steps
+    copies = [
+        pltpu.make_async_copy(down, down_out, sems.at[0]),
+        pltpu.make_async_copy(gate, gate_out, sems.at[1]),
+    ]
+
+    @pl.when(i == 0)
+    def _():
+        for copy in copies:
+            copy.start()
+
+    cols = pl.ds(pl.multiple_of(i * out.shape[0], out.shape[0]), out.shape[0])
+    out[...] = lax.dot_general(
+        lhs[:, :, cols].reshape(rhs.shape[0], out.shape[0]), rhs[...], CONTRACT_ROWS, preferred_element_type=F32
+    ).astype(BF16)
+
+    @pl.when(i == steps - 1)
+    def _():
+        for copy in copies:
+            copy.wait()
+
+
+def last_grad(act, gup, down, gate):
+    cols, shard, width = act.shape
+    tokens, feats = gup.shape
+    tile = tile_of(width, 512)
+    steps = width // tile
     sds = jax.ShapeDtypeStruct
     vmem = pl.BlockSpec(memory_space=pltpu.VMEM)
+    hbm = pl.BlockSpec(memory_space=pltpu.HBM)
     return pl.pallas_call(
-        functools.partial(grads_kernel, steps),
+        functools.partial(last_kernel, steps),
         grid=(steps,),
-        out_shape=[sds((feats, width), BF16), sds((width, feats), BF16), sds((width, feats), BF16)],
+        out_shape=[sds((width, feats), BF16), sds(down.shape, BF16), sds(gate.shape, BF16)],
         in_specs=[
-            pl.BlockSpec((tokens, ft), lambda i: (0, i)),
-            pl.BlockSpec((cols, shard, width), lambda i: (0, 0, 0)),
-            pl.BlockSpec((tokens, feats), lambda i: (0, 0)),
-            pl.BlockSpec((tokens, feats), lambda i: (0, 0)),
-            pl.BlockSpec((cols, shard, wt), lambda i: (0, 0, i)),
+            vmem,
+            vmem,
+            vmem,
+            vmem,
         ],
-        out_specs=[
-            pl.BlockSpec((ft, width), lambda i: (i, 0)),
-            pl.BlockSpec((wt, feats), lambda i: (i, 0)),
-            pl.BlockSpec((wt, feats), lambda i: (i, 0)),
-        ],
-        name="weight_grads",
-    )(hid, go, ggp, gup, act)
+        out_specs=[pl.BlockSpec((tile, feats), lambda i: (i, 0)), hbm, hbm],
+        scratch_shapes=[pltpu.SemaphoreType.DMA((2,))],
+        compiler_params=pltpu.CompilerParams(vmem_limit_bytes=16 << 20),
+        name="last_grad",
+    )(*(pltpu.with_memory_space_constraint(x, pltpu.VMEM) for x in (act, gup, down, gate)))
 
 
 def local(row_size, col_size, activations, grad_output, gate_pre, up_pre, w_gate, w_up, w_down):
-    grad_input, go_all, act_all, hid, ggp, gup = exchange(
+    grad_input, grad_down, grad_gate, act_all, gup = exchange(
         row_size, col_size, activations, grad_output, gate_pre, up_pre, w_gate, w_up, w_down
     )
-    grad_down, grad_gate, grad_up = weight_grads(hid, go_all, act_all, ggp, gup)
+    grad_up, grad_down, grad_gate = last_grad(act_all, gup, grad_down, grad_gate)
     return grad_input, grad_gate, grad_up, grad_down
 
 

time: 133 us -> 117 us (0.88)
  Pallas kernels: 131 us -> 115 us
    pallas_call x1, Pallas kernels: 112 us -> 103 us  [exchange(): pl.pallas_call(functools.partial(exchange_kernel, row_size, col_size), ou...]
    pallas_call x1, Pallas kernels: 19 us -> 12.2 us  [last_grad(): pl.pallas_call(functools.partial(last_kernel, steps), grid=(steps,), out_...]
where the time goes in v1:
time: 117 us
  Pallas kernels  115 us (98%)
    pallas_call x1, Pallas kernels, exchange(): pl.pallas_call(functools.partial(exchange_kernel, row_size, col_size), ou...  103 us
    pallas_call x1, Pallas kernels, last_grad(): pl.pallas_call(functools.partial(last_kernel, steps), grid=(steps,), out_...  12.2 us

profile of v1, /device:TPU:0, one launch (start us, length us, event | category | flops | bytes accessed | tf_op | source)
XLA Modules:
  0.0 116.7 jit_solution(15712642729043968908)
XLA Ops:
  0.6 103.0 %exchange.1 = (bf16[64,4096]{1,0:T(8,128)(2,1)}, bf16[1024,4096]{1,0:T(8,128)(2,1)S(1)}, bf16[4096,1024]{1,0:T(8,128)(2,1)S(1)}, bf16[8,64,4096]{2,1,0:T(8,128)(2,1)S(1)}, bf16[512,1024]{1,0:T(8,128)(2,1)S(1)}) custom-call(bf16[64,4096]{1,0:T(8,128)(2,1)} %act_hbm.1, bf16[64,4096]{1,0:T(8,128)(2,1)} %go_hbm.1, bf16[128,1024]{1,0:T(8,128)(2,1)} %gate_hbm.1, ...), custom_call_target="tpu_custom_call" | custom-call | tf_op jit(solution)/shard_map/exchange/pallas_call | solution.py:534
  103.6 0.0 copy-start
  103.7 12.2 %last_grad.1 = (bf16[4096,1024]{1,0:T(8,128)(2,1)}, bf16[1024,4096]{1,0:T(8,128)(2,1)}, bf16[4096,1024]{1,0:T(8,128)(2,1)}) custom-call(bf16[8,64,4096]{2,1,0:T(8,128)(2,1)S(1)} %get-tuple-element.13.lhs, bf16[512,1024]{1,0:T(8,128)(2,1)S(1)} %get-tuple-element.14.rhs, bf16[1024,4096]{1,0:T(8,128)(2,1)S(1)} %get-tuple-element.15.down, ...), custom_call_target="tpu_custom_call" | custom-call | tf_op jit(solution)/shard_map/last_grad/pallas_call | solution.py:606
  115.9 0.0 copy-done
  115.9 0.8 copy.12
Async XLA Ops:
  103.6 12.2 %copy-start = (bf16[64,4096]{1,0:T(8,128)(2,1)S(1)}, bf16[64,4096]{1,0:T(8,128)(2,1)}, u32[]{:S(2)}) copy-start(bf16[64,4096]{1,0:T(8,128)(2,1)} %get-tuple-element.24) | copy-start | bytes 1572868

commit v2 on v1

--- a/solution.py
+++ b/solution.py
@@ -240,12 +240,12 @@
             res = lax.dot_general(lhs, wd[cols, :], CONTRACT_COLS, preferred_element_type=F32)
             part32[:, cols] = res
             part16[ds(j * chunk, chunk), cols] = res.astype(BF16)
+            for d in range(1, R):
+                src = part16.at[ds(j * chunk + peer(d) * own_rows, own_rows), cols]
+                dst = rs_in.at[ds((j * (R - 1) + d - 1) * own_rows, own_rows), cols]
+                remote(src, dst, rs_s.at[j], rs_r.at[j], (peer(d), c)).start()
 
         own32[ds(j * own_rows, own_rows), :] = part32[ds(r * own_rows, own_rows), :]
-        for d in range(1, R):
-            src = part16.at[ds(j * chunk + peer(d) * own_rows, own_rows), :]
-            dst = rs_in.at[ds((j * (R - 1) + d - 1) * own_rows, own_rows), :]
-            remote(src, dst, rs_s.at[j], rs_r.at[j], (peer(d), c)).start()
 
     def finish_sum(j):
         rows_wait(rs_in, rs_s.at[j], rs_r.at[j], (R - 1) * own_rows).wait_recv()
@@ -284,9 +284,125 @@
         if s > 0:
             pl.when(z + s < Z)(lambda: step(z + s))
 
+    gtile = tile_of(wt, 256)
+
+    half_line = Z // 2
+    first = jnp.where(lower, 0, half_line)
+    last = jnp.where(lower, half_line, 0)
+
+    def input_tile(n, start, count):
+        rows_at = ds(start * chunk, count * chunk, chunk)
+
+        @pl.loop(0, wt // gtile)
+        def _(t):
+            at = ds(n * wt + t * gtile, gtile)
+            res = lax.dot_general(ggp_all[rows_at, :], wg[at, :], CONTRACT_COLS, preferred_element_type=F32)
+            res = res + lax.dot_general(gup_all[rows_at, :], wu[at, :], CONTRACT_COLS, preferred_element_type=F32)
+            for j in range(count):
+                for side in range(2):
+                    low_row = (2 * j + side) * shard
+                    gi[n, side, start + j, :, ds(t * gtile, gtile)] = res[low_row : low_row + shard]
+
+    def pair_sum(n, late):
+        at = pl.ds(last if late else first, half_line)
+        return remote(gi.at[n, 1 - k, at], pair_in.at[n, at], pr_s.at[late, n], pr_r.at[late, n], partner)
+
+    def early(n):
+        input_tile(n, first, half_line)
+        pair_sum(n, 0).start()
+
+    def late(n):
+        input_tile(n, last, half_line)
+        pair_sum(n, 1).start()
+
+    def z_copy(n, j, slot, dev):
+        return remote(z_out.at[n, j], z_in.at[n, slot], z_s.at[n, j], z_r.at[n, slot], dev)
+
+    def pass_on(n, j, fed, slot, dev):
+        total = gi[n, k, j] + pair_in[n, j]
+        if fed:
+            z_copy(n, j, j, dev).wait_recv()
+            total = total + z_in[n, j].astype(F32)
+        z_out[n, j] = total.astype(BF16)
+        z_copy(n, j, slot, dev).start()
+
+    def move_up(n, j, fed):
+        pass_on(n, j, fed, j, above)
+
+    def move_down(n, j, fed):
+        pass_on(n, j, fed, jnp.where(z - 1 == j, Z, j), below)
+
+    def edge_serve(n, is_late):
+        pair_sum(n, is_late).wait_recv()
+        for j in range(Z - 1, half_line - 1, -1) if is_late else range(half_line - 1, 0, -1):
+            pl.when(lower)(functools.partial(move_up, n, j, False))
+        for j in range(half_line) if is_late else range(half_line, Z - 1):
+            pl.when(jnp.logical_not(lower))(functools.partial(move_down, n, j, False))
+
+    def mid_early(n):
+        pair_sum(n, 0).wait_recv()
+        for j in range(half_line - 1, 1, -1):
+            pl.when((z < j) & lower)(functools.partial(move_up, n, j, True))
+        for j in range(half_line, Z - 2):
+            pl.when((z > j) & jnp.logical_not(lower))(functools.partial(move_down, n, j, True))
+
+    def mid_late(n, near):
+        if near:
+            pair_sum(n, 1).wait_recv()
+        for j in range(Z - 1, half_line - 1, -1):
+            pl.when((z < j) & (lower == near))(functools.partial(move_up, n, j, True))
+        for j in range(half_line):
+            pl.when((z > j) & (lower != near))(functools.partial(move_down, n, j, True))
+
+    def finish(n):
+        total = gi[n, k, z] + pair_in[n, z]
+        cols = pl.ds(n * wt, wt)
+        gi[n, k, z] = total
+
+        @pl.when(has_dn)
+        def _():
+            z_copy(n, z, z, below).wait_recv()
+            gi[n, k, z] += z_in[n, z].astype(F32)
+
+        @pl.when(has_up)
+        def _():
+            z_copy(n, z, Z, above).wait_recv()
+            gi[n, k, z] += z_in[n, Z].astype(F32)
+
+        gi_out[:, cols] = gi[n, k, z].astype(BF16)
+
+    blocks = 4
+    fb = feats // blocks
+    wb = width // blocks
+    nb = tile_of(width, 1024)
+
+    def down_block(i):
+        rows_at = pl.ds(i * fb, fb)
+
+        @pl.loop(0, width // nb)
+        def _(t):
+            cols = ds(t * nb, nb)
+            rhs = go_all[:, :, cols].reshape(tokens, nb)
+            wd[rows_at, cols] = lax.dot_general(
+                hid_all[:, rows_at], rhs, CONTRACT_ROWS, preferred_element_type=F32
+            ).astype(BF16)
+
+    def gate_block(i):
+        gb = tile_of(wb, 256)
+
+        @pl.loop(0, wb // gb)
+        def _(t):
+            cols = ds(i * wb + t * gb, gb)
+            lhs = act_all[:, :, cols].reshape(tokens, gb)
+            wg[cols, :] = lax.dot_general(
+                lhs, ggp_all[...], CONTRACT_ROWS, preferred_element_type=F32
+            ).astype(BF16)
+
     for s in range(Z):
         if s > 0:
             forward(s)
+        if s == half_line + 1:
+            pl.when(edge)(lambda: early(1))
         if s == 0:
             loads[3].wait()
         at_distance(s, partial_hidden)
@@ -296,196 +412,96 @@
             act_relay(s)
         if s > 0:
             pl.when(jnp.logical_not(edge))(lambda: at_distance(s - 1, finish_sum))
-        if s == 2:
+        if s == min(2, Z - 1):
             gathered_saved()
             at_distance(0, finish_gather)
-            pl.when(edge)(lambda: at_distance(1, finish_gather))
+            if Z > 2:
+                pl.when(edge)(lambda: at_distance(1, finish_gather))
+            loads[5].wait()
+            loads[6].wait()
         if s > 2:
             pl.when(jnp.logical_not(edge))(lambda: at_distance(s - 2, finish_gather))
-            pl.when(edge)(lambda: at_distance(s - 1, finish_gather))
+            if s < Z - 1:
+                pl.when(edge)(lambda: at_distance(s - 1, finish_gather))
+        if s == half_line:
+            pl.when(edge)(lambda: early(0))
         if s < Z - 1:
             pl.when(edge)(lambda: at_distance(s, finish_sum))
-    if Z == 2:
-        gathered_saved()
-        at_distance(0, finish_gather)
+        if s == half_line:
+            pl.when(edge)(lambda: edge_serve(0, 0))
+
     if Z > 2:
         pl.when(jnp.logical_not(edge))(lambda: at_distance(Z - 2, finish_gather))
 
-    loads[5].wait()
-    loads[6].wait()
-    gtile = tile_of(wt, 256)
-
-    first = jnp.where(lower, 0, 1)
-    last = jnp.where(lower, Z - 1, 0)
-
-    def input_tile(n, start, count):
-        rows_at = ds(start * chunk, count * chunk, chunk)
-
-        @pl.loop(0, wt // gtile)
-        def _(t):
-            at = ds(n * wt + t * gtile, gtile)
-            res = lax.dot_general(ggp_all[rows_at, :], wg[at, :], CONTRACT_COLS, preferred_element_type=F32)
-            res = res + lax.dot_general(gup_all[rows_at, :], wu[at, :], CONTRACT_COLS, preferred_element_type=F32)
-            for j in range(count):
-                for side in range(2):
-                    low_row = (2 * j + side) * shard
-                    gi[n, side, start + j, :, ds(t * gtile, gtile)] = res[low_row : low_row + shard]
-
-    def pair_sum(n, late):
-        at = pl.ds(last, 1) if late else pl.ds(first, Z - 1)
-        return remote(gi.at[n, 1 - k, at], pair_in.at[n, at], pr_s.at[late, n], pr_r.at[late, n], partner)
-
-    def early(n):
-        input_tile(n, first, Z - 1)
-        pair_sum(n, 0).start()
-
-    def late(n):
-        input_tile(n, last, 1)
-        pair_sum(n, 1).start()
-
-    def z_copy(n, j, slot, dev):
-        return remote(z_out.at[n, j], z_in.at[n, slot], z_s.at[n, j], z_r.at[n, slot], dev)
-
-    def pass_on(n, j, fed, slot, dev):
-        total = gi[n, k, j] + pair_in[n, j]
-        if fed:
-            z_copy(n, j, j, dev).wait_recv()
-            total = total + z_in[n, j].astype(F32)
-        z_out[n, j] = total.astype(BF16)
-        z_copy(n, j, slot, dev).start()
-
-    def move_up(n, j, fed):
-        pass_on(n, j, fed, j, above)
-
-    def move_down(n, j, fed):
-        pass_on(n, j, fed, jnp.where(z - 1 == j, Z, j), below)
-
-    def edge_serve(n, is_late):
-        pair_sum(n, is_late).wait_recv()
-        for j in [Z - 1] if is_late else range(Z - 2, 0, -1):
-            pl.when(lower)(functools.partial(move_up, n, j, False))
-        for j in [0] if is_late else range(1, Z - 1):
-            pl.when(jnp.logical_not(lower))(functools.partial(move_down, n, j, False))
-
-    def mid_early(n):
-        pair_sum(n, 0).wait_recv()
-
-        def ups(side):
-            for j in range(Z - 2, 1, -1):
-                pl.when((z < j) & (lower == side))(functools.partial(move_up, n, j, True))
-
-        ups(True)
-        for j in range(1, Z - 2):
-            pl.when(z > j)(functools.partial(move_down, n, j, True))
-        ups(False)
-
-    def mid_late(n, near):
-        if near:
-            pair_sum(n, 1).wait_recv()
-        pl.when(lower == near)(functools.partial(move_up, n, Z - 1, True))
-        pl.when(lower != near)(functools.partial(move_down, n, 0, True))
-
-    def finish(n):
-        total = gi[n, k, z] + pair_in[n, z]
-        cols = pl.ds(n * wt, wt)
-        gi[n, k, z] = total
-
-        @pl.when(has_dn)
-        def _():
-            z_copy(n, z, z, below).wait_recv()
-            gi[n, k, z] += z_in[n, z].astype(F32)
-
-        @pl.when(has_up)
-        def _():
-            z_copy(n, z, Z, above).wait_recv()
-            gi[n, k, z] += z_in[n, Z].astype(F32)
-
-        gi_out[:, cols] = gi[n, k, z].astype(BF16)
-
-    blocks = 4
-    fb = feats // blocks
-    wb = width // blocks
-    nb = tile_of(width, 1024)
-
-    def down_block(i):
-        rows_at = pl.ds(i * fb, fb)
-
-        @pl.loop(0, width // nb)
-        def _(t):
-            cols = ds(t * nb, nb)
-            rhs = go_all[:, :, cols].reshape(tokens, nb)
-            wd[rows_at, cols] = lax.dot_general(
-                hid_all[:, rows_at], rhs, CONTRACT_ROWS, preferred_element_type=F32
-            ).astype(BF16)
-
-    def gate_block(i):
-        gb = tile_of(wb, 256)
-
-        @pl.loop(0, wb // gb)
-        def _(t):
-            cols = ds(i * wb + t * gb, gb)
-            lhs = act_all[:, :, cols].reshape(tokens, gb)
-            wg[cols, :] = lax.dot_general(
-                lhs, ggp_all[...], CONTRACT_ROWS, preferred_element_type=F32
-            ).astype(BF16)
-
-    early(0)
-
     @pl.when(edge)
     def _():
-        edge_serve(0, 0)
+        if half_line + 1 >= Z:
+            early(1)
+        edge_serve(1, 0)
+        if Z > 3:
+            at_distance(Z - 2, finish_gather)
+        early(2)
         at_distance(Z - 1, finish_sum)
-        early(1)
+        edge_serve(2, 0)
+        early(3)
+        edge_serve(3, 0)
         at_distance(Z - 1, finish_gather)
         late(0)
+        edge_serve(0, 1)
         for n in range(1, ntiles):
-            edge_serve(n, 0)
-            edge_serve(n - 1, 1)
-            if n + 1 < ntiles:
-                early(n + 1)
             late(n)
-        edge_serve(ntiles - 1, 1)
+            edge_serve(n, 1)
+        for s in range(1, Z - 1):
+            act_end(s)
+        for i in range(blocks):
+            down_block(i)
+        act_end(Z - 1)
+        for j in range(Z):
+            act_pair(j, 1 - k).wait_recv()
+        for i in range(blocks):
+            gate_block(i)
 
     @pl.when(jnp.logical_not(edge))
     def _():
         at_distance(Z - 1, finish_sum)
-        mid_early(0)
+        early(0)
         act_relay(Z)
-        early(1)
         at_distance(Z - 1, finish_gather)
         late(0)
-        for n in range(1, ntiles):
-            if n + 1 < ntiles:
-                early(n + 1)
-            mid_early(n)
-            late(n)
-            down_block(n - 1)
-            mid_late(n - 1, True)
-            if n > 1:
-                mid_late(n - 2, False)
-            act_relay(Z + n)
-        for n in (ntiles - 1, ntiles):
-            if n < ntiles:
-                down_block(n)
-                mid_late(n, True)
-            mid_late(n - 1, False)
-        for t in range(Z + ntiles, 2 * Z - 2):
+        early(1)
+        late(1)
+        mid_early(0)
+        mid_early(1)
+        early(2)
+        late(2)
+        mid_early(2)
+        down_block(0)
+        down_block(1)
+        mid_late(0, True)
+        act_relay(Z + 1)
+        early(3)
+        late(3)
+        mid_early(3)
+        mid_late(1, True)
+        mid_late(0, False)
+        for t in range(Z + 2, 2 * Z - 2):
             act_relay(t)
-
-    for s in range(1, Z):
-        act_end(s)
-    for j in range(Z):
-        act_pair(j, 1 - k).wait_recv()
-
-    @pl.when(edge)
-    def _():
-        for i in range(blocks):
-            down_block(i)
+        down_block(2)
+        down_block(3)
+        mid_late(2, True)
+        mid_late(1, False)
+        for j in range(Z):
+            act_pair(j, 1 - k).wait_recv()
+        gate_block(0)
+        gate_block(1)
+        mid_late(3, True)
+        mid_late(2, False)
+        gate_block(2)
+        mid_late(3, False)
+        gate_block(3)
 
     for n in range(ntiles):
         finish(n)
-        for i in range(n * blocks // ntiles, (n + 1) * blocks // ntiles):
-            gate_block(i)
 
     for j in range(Z):
         go_pair(j, k).wait_send()
@@ -534,7 +550,7 @@
     return pl.pallas_call(
         functools.partial(exchange_kernel, row_size, col_size),
         out_shape=[
-            sds((shard, width), BF16),
+            pltpu.VMEM((shard, width), BF16),
             pltpu.VMEM(wd.shape, BF16),
             pltpu.VMEM(wg.shape, BF16),
             pltpu.VMEM((col_size, shard, width), BF16),
@@ -572,17 +588,17 @@
     )(*(pltpu.with_memory_space_constraint(x, pltpu.HBM) for x in (act, go, gate, up, wg, wu, wd)))
 
 
-def last_kernel(steps, lhs, rhs, down, gate, out, down_out, gate_out, sems):
+def last_kernel(steps, lhs, rhs, down, gate, inp, out, down_out, gate_out, inp_out, sems):
     i = pl.program_id(0)
-    copies = [
-        pltpu.make_async_copy(down, down_out, sems.at[0]),
-        pltpu.make_async_copy(gate, gate_out, sems.at[1]),
-    ]
-
-    @pl.when(i == 0)
-    def _():
-        for copy in copies:
-            copy.start()
+
+    def copies(step):
+        for a, (src, dst) in enumerate(((down, down_out), (gate, gate_out), (inp, inp_out))):
+            part = src.shape[0] // steps
+            at = pl.ds(pl.multiple_of(step * part, part), part)
+            yield pltpu.make_async_copy(src.at[at], dst.at[at], sems.at[a, step])
+
+    for copy in copies(i):
+        copy.start()
 
     cols = pl.ds(pl.multiple_of(i * out.shape[0], out.shape[0]), out.shape[0])
     out[...] = lax.dot_general(
@@ -591,11 +607,12 @@
 
     @pl.when(i == steps - 1)
     def _():
-        for copy in copies:
-            copy.wait()
-
-
-def last_grad(act, gup, down, gate):
+        for step in range(steps):
+            for copy in copies(step):
+                copy.wait()
+
+
+def last_grad(act, gup, down, gate, inp):
     cols, shard, width = act.shape
     tokens, feats = gup.shape
     tile = tile_of(width, 512)
@@ -606,25 +623,26 @@
     return pl.pallas_call(
         functools.partial(last_kernel, steps),
         grid=(steps,),
-        out_shape=[sds((width, feats), BF16), sds(down.shape, BF16), sds(gate.shape, BF16)],
+        out_shape=[sds(x, BF16) for x in ((width, feats), down.shape, gate.shape, inp.shape)],
         in_specs=[
             vmem,
             vmem,
             vmem,
             vmem,
+            vmem,
         ],
-        out_specs=[pl.BlockSpec((tile, feats), lambda i: (i, 0)), hbm, hbm],
-        scratch_shapes=[pltpu.SemaphoreType.DMA((2,))],
+        out_specs=[pl.BlockSpec((tile, feats), lambda i: (i, 0)), hbm, hbm, hbm],
+        scratch_shapes=[pltpu.SemaphoreType.DMA((3, steps))],
         compiler_params=pltpu.CompilerParams(vmem_limit_bytes=16 << 20),
         name="last_grad",
-    )(*(pltpu.with_memory_space_constraint(x, pltpu.VMEM) for x in (act, gup, down, gate)))
+    )(*(pltpu.with_memory_space_constraint(x, pltpu.VMEM) for x in (act, gup, down, gate, inp)))
 
 
 def local(row_size, col_size, activations, grad_output, gate_pre, up_pre, w_gate, w_up, w_down):
     grad_input, grad_down, grad_gate, act_all, gup = exchange(
         row_size, col_size, activations, grad_output, gate_pre, up_pre, w_gate, w_up, w_down
     )
-    grad_up, grad_down, grad_gate = last_grad(act_all, gup, grad_down, grad_gate)
+    grad_up, grad_down, grad_gate, grad_input = last_grad(act_all, gup, grad_down, grad_gate, grad_input)
     return grad_input, grad_gate, grad_up, grad_down
 
 

time: 117 us -> 103 us (0.88)
  Pallas kernels: 115 us -> 102 us
    pallas_call x1, Pallas kernels: 103 us -> 92.7 us  [exchange(): pl.pallas_call(functools.partial(exchange_kernel, row_size, col_size), ou...]
    pallas_call x1, Pallas kernels: 12.2 us -> 9.57 us  [last_grad(): pl.pallas_call(functools.partial(last_kernel, steps), grid=(steps,), out_...]
where the time goes in v2:
time: 103 us
  Pallas kernels  102 us (99%)
    pallas_call x1, Pallas kernels, exchange(): pl.pallas_call(functools.partial(exchange_kernel, row_size, col_size), ou...  92.7 us
    pallas_call x1, Pallas kernels, last_grad(): pl.pallas_call(functools.partial(last_kernel, steps), grid=(steps,), out_...  9.57 us

profile of v2, /device:TPU:0, one launch (start us, length us, event | category | flops | bytes accessed | tf_op | source)
XLA Modules:
  0.0 103.1 jit_solution(898618539787647249)
XLA Ops:
  0.6 92.7 %exchange.1 = (bf16[64,4096]{1,0:T(8,128)(2,1)S(1)}, bf16[1024,4096]{1,0:T(8,128)(2,1)S(1)}, bf16[4096,1024]{1,0:T(8,128)(2,1)S(1)}, bf16[8,64,4096]{2,1,0:T(8,128)(2,1)S(1)}, bf16[512,1024]{1,0:T(8,128)(2,1)S(1)}) custom-call(bf16[64,4096]{1,0:T(8,128)(2,1)} %act_hbm.1, bf16[64,4096]{1,0:T(8,128)(2,1)} %go_hbm.1, bf16[128,1024]{1,0:T(8,128)(2,1)} %gate_hbm.1, ...), custom_call_target="tpu_custom_call" | custom-call | tf_op jit(solution)/shard_map/exchange/pallas_call | solution.py:550
  93.4 9.6 %last_grad.1 = (bf16[4096,1024]{1,0:T(8,128)(2,1)}, bf16[1024,4096]{1,0:T(8,128)(2,1)}, bf16[4096,1024]{1,0:T(8,128)(2,1)}, bf16[64,4096]{1,0:T(8,128)(2,1)}) custom-call(bf16[8,64,4096]{2,1,0:T(8,128)(2,1)S(1)} %get-tuple-element.13.lhs, bf16[512,1024]{1,0:T(8,128)(2,1)S(1)} %get-tuple-element.14.rhs, bf16[1024,4096]{1,0:T(8,128)(2,1)S(1)} %get-tuple-element.15.down, ...), custom_call_target="tpu_custom_call" | custom-call | tf_op jit(solution)/shard_map/last_grad/pallas_call | solution.py:623
